TPU v7x, 32 devices: a whole 2x2x4 slice. The times are simulated.
32 devices in a mesh: space: 8 (over y, x, core), tm: 4 (over z).
Axes of the slice: x: 2, y: 2, z: 4, core: 2. Of those that a mesh axis runs over, the one named last changes fastest.
Arguments:
- series: bfloat16 [16384, 2, 512], P('space', None, 'tm'), may hold values from -6 to 6
- space_basis: bfloat16 [16384, 16384], P('space', 'tm'), may hold values from -0.046875 to 0.046875
- time_basis: bfloat16 [512, 512], P('tm'), may hold values from -0.25 to 0.25
- space_eig: float32 [16384], replicated, may hold values from 0.3 to 3
- time_eig: float32 [512], replicated, may hold values from 0.3 to 3
Outputs:
- alpha: bfloat16 [16384, 2, 512], P('space', None, 'tm')
- grad_space: bfloat16 [16384, 8, 2048], P('space', None, 'tm')
All inputs are finite; a program needn't handle non-finite values.
Results may differ from a plain program's by a relative error of at most 0.0063.
Values may be sent and summed in bfloat16 or wider, within the bound.
A program may use at most 128 MiB of HBM per device.

v0:
```python
import jax
import jax.numpy as jnp
from jax import lax
from jax.sharding import PartitionSpec as P

TIMES = 512
REPS = 2


def scale_block(spectral, eig_rows, eig_cols):
    denom = eig_rows[:, None] * eig_cols[None, :] + 0.1
    return (spectral / denom).astype(jnp.bfloat16)


def per_device(series, space_basis, time_basis, space_eig, time_eig):
    space_count = lax.axis_size("space")
    time_count = lax.axis_size("tm")
    time_idx = lax.axis_index("tm")
    row_count = space_basis.shape[0]
    col_block = space_basis.shape[1]
    time_local = time_basis.shape[0]
    wide_cols = REPS * TIMES
    sub_rows = row_count // time_count
    cols_tiled = jnp.tile(time_eig, REPS)
    full_series, full_basis = (
        lax.all_gather(series, "tm", axis=2, tiled=True),
        lax.all_gather(time_basis, "tm", axis=0, tiled=True),
    )
    rotated = jnp.dot(
        full_series.reshape(row_count * REPS, TIMES), full_basis, preferred_element_type=jnp.float32
    ).astype(jnp.bfloat16)
    rotated = rotated.reshape(row_count, wide_cols)
    contract_rows = (((0,), (0,)), ((), ()))
    partial_spec = lax.dot_general(
        space_basis, rotated, contract_rows, preferred_element_type=jnp.float32
    )
    spectral = lax.psum(partial_spec, "space")
    eig_rows = lax.dynamic_slice_in_dim(space_eig, time_idx * col_block, col_block)
    scaled_spec = scale_block(spectral, eig_rows, cols_tiled)
    back_part = jnp.dot(space_basis, scaled_spec, preferred_element_type=jnp.float32)
    back_all = lax.psum(back_part, "tm").astype(jnp.bfloat16)
    back_sub = lax.dynamic_slice_in_dim(back_all, time_idx * sub_rows, sub_rows, 0)
    contract_last = (((1,), (1,)), ((), ()))
    alpha = lax.dot_general(
        back_all.reshape(row_count * REPS, TIMES),
        time_basis,
        contract_last,
        preferred_element_type=jnp.float32,
    )
    alpha = alpha.astype(jnp.bfloat16).reshape(row_count, REPS, time_local)
    weighted = (
        back_all.reshape(row_count, REPS, TIMES).astype(jnp.float32) * time_eig[None, None, :]
    )
    weighted = (weighted / (REPS * TIMES)).astype(jnp.bfloat16).reshape(row_count, wide_cols)
    grad = lax.dot_general(
        weighted,
        lax.all_gather(back_sub, "space", axis=0, tiled=True),
        contract_last,
        preferred_element_type=jnp.float32,
    )
    grad = grad.astype(jnp.bfloat16).reshape(row_count, space_count, sub_rows)
    return (alpha, grad)


def solution(mesh):
    return jax.shard_map(
        per_device,
        mesh=mesh,
        in_specs=(P("space", None, "tm"), P("space", "tm"), P("tm", None), P(), P()),
        out_specs=(P("space", None, "tm"), P("space", None, "tm")),
        check_vma=False,
    )
```

profile of v0, /device:TPU:0, one launch (start us, length us, event | category | flops | bytes accessed | tf_op | source)
XLA Modules:
  0.0 778.3 jit_solution(7455162140651493963)
XLA Ops:
  7.2 0.0 copy-start
  7.2 0.0 all-gather.3.cloned.1.call-start
  7.2 0.7 all-gather.3.cloned.1.call-update
  7.9 0.0 all-reduce.3.cloned.1.call-start
  8.0 19.0 %all_gather.10 = bf16[512,512]{1,0:T(8,128)(2,1)S(1)} all-gather(bf16[128,512]{1,0:T(8,128)(2,1)} %param.7), channel_id=1, replica_groups=mesh['space'=8,'tm'=4] {'tm'}, dimensions={0}, use_global_device_ids=true | all-gather | bytes 655360 | tf_op jit(solution)/shard_map/all_gather | solution.py:27
  27.0 70.6 %all-gather.3.cloned.1.call-done = bf16[2048,2,512]{2,1,0:T(2,128)(2,1)} async-done(((bf16[2048,2,128]{2,1,0:T(2,128)(2,1)}), bf16[2048,2,512]{2,1,0:T(2,128)(2,1)}) %all-gather.3.cloned.1.call-update) | async-done | bytes 4194320 | tf_op jit(solution)/shard_map/all_gather | solution.py:26
  97.5 7.2 reshape.26
  104.7 6.5 convolution_convert_fusion.1
  111.2 7.1 reshape.27
  118.3 23.8 %convolution_bitcast_fusion = f32[4096,1024]{0,1:T(8,128)} fusion(bf16[2048,1024]{1,0:T(8,128)(2,1)} %reshape.27, bf16[2048,4096]{1,0:T(8,128)(2,1)} %param.6), kind=kOutput, calls=%fused_computation.2 | convolution fusion | flops 17179869184 | bytes 37748736 | tf_op jit(solution)/shard_map/dot_general | solution.py:34
  142.1 0.0 all-reduce.3.cloned.1.call-update
  142.2 0.0 all-gather.5.cloned.1.call-start
  142.2 0.7 dynamic_slice.6
  143.0 216.2 %all-reduce.3.cloned.1.call-done = f32[4096,1024]{0,1:T(8,128)} async-done(((f32[4096,1024]{0,1:T(8,128)}), f32[4096,1024]{0,1:T(8,128)}) %all-reduce.3.cloned.1.call-update) | async-done | bytes 16777232 | tf_op jit(solution)/shard_map/psum | solution.py:37
  359.2 26.6 %fusion.1 = f32[2048,1024]{0,1:T(8,128)} fusion(bf16[2048,4096]{1,0:T(8,128)(2,1)} %param.6, f32[4096,1024]{0,1:T(8,128)} %all-reduce.3.cloned.1.call-done, f32[1024]{0:T(1024)S(1)} %bitcast.21, f32[4096]{0:T(1024)S(1)} %dynamic_slice.6), kind=kOutput, calls=%fused_computation.7 | convolution fusion | flops 17196646400 | bytes 41963520 | tf_op jit(solution)/shard_map/dot_general | solution.py:40
  385.8 284.3 %all-reduce.4 = bf16[2048,1024]{0,1:T(8,128)(2,1)} all-reduce(f32[2048,1024]{0,1:T(8,128)} %fusion.1), channel_id=1, replica_groups=mesh['space'=8,'tm'=4] {'tm'}, use_global_device_ids=true, to_apply=%region_1.0 | all-reduce | flops 2097152 | bytes 12582912 | tf_op jit(solution)/shard_map/psum | solution.py:41
  670.1 2.3 constant_dynamic-slice_fusion
  672.4 0.0 all-gather.5.cloned.1.call-update
  672.4 6.4 copy.7
  678.9 7.2 reshape.28
  686.1 4.4 convolution_convert_fusion.2
  690.5 39.1 %all-gather.5.cloned.1.call-done = bf16[4096,1024]{0,1:T(8,128)(2,1)} async-done(((bf16[512,1024]{0,1:T(8,128)(2,1)}), bf16[4096,1024]{0,1:T(8,128)(2,1)}) %all-gather.5.cloned.1.call-update) | async-done | bytes 8388624 | tf_op jit(solution)/shard_map/all_gather | solution.py:57
  729.6 25.5 %convolution_convert_fusion = bf16[2048,4096]{1,0:T(8,128)(2,1)} fusion(bf16[4096,1024]{0,1:T(8,128)(2,1)} %all-gather.5.cloned.1.call-done, bf16[2048,1024]{0,1:T(8,128)(2,1)} %all-reduce.4, f32[1024]{0:T(1024)S(1)} %bitcast.22), kind=kOutput, calls=%fused_computation.1 | convolution fusion | flops 17196646400 | bytes 29364224 | tf_op jit(solution)/shard_map/dot_general | solution.py:55
  755.1 16.6 %copy.9 = bf16[256,8,8,512]{3,2,1,0:T(8,128)(2,1)} copy(bf16[256,8,8,512]{3,1,2,0:T(8,128)(2,1)} %bitcast.19) | data formatting | bytes 33554432
  (7 shorter events, 0.0 us)
Async XLA Ops:
  7.2 135.1 %copy-start = (f32[512]{0:T(512)S(1)}, f32[512]{0:T(512)}, u32[]{:S(2)}) copy-start(f32[512]{0:T(512)} %param.9) | copy-start | bytes 6148
  7.2 90.4 %all-gather.3.cloned.1.call-start = ((), (), s32[]{:S(2)}) async-start(), calls=%async_computation | async-start | bytes 5242880 | tf_op jit(solution)/shard_map/all_gather | solution.py:26
  7.9 351.3 %all-reduce.3.cloned.1.call-start = ((), (), s32[]{:S(2)}) async-start(), calls=%async_computation.1 | async-start | bytes 33554432 | tf_op jit(solution)/shard_map/psum | solution.py:37
  142.2 587.5 %all-gather.5.cloned.1.call-start = ((), (), s32[]{:S(2)}) async-start(), calls=%async_computation.2 | async-start | bytes 9437184 | tf_op jit(solution)/shard_map/all_gather | solution.py:57
  672.4 13.7 %copy-start.2 = (bf16[128,512]{1,0:T(8,128)(2,1)S(1)}, bf16[128,512]{1,0:T(8,128)(2,1)}, u32[]{:S(2)}) copy-start(bf16[128,512]{1,0:T(8,128)(2,1)} %param.7) | copy-start | bytes 393220
  755.1 16.6 %copy-start.1 = (f32[512]{0:T(512)S(1)}, f32[512]{0:T(512)}, u32[]{:S(2)}) copy-start(f32[512]{0:T(512)} %param.9) | copy-start | bytes 6148
Sparse Core Ops, SparseCore 0:
  9.5 87.9 all-gather.2
  142.3 216.8 all-reduce.2
  672.6 57.0 all-gather.4
where the time goes:
time: 779 us; the launch traced here: 778 us
  waiting for transfers between devices  327 us (42%)
  blocking collectives  303 us (39%)
  matrix products  86.8 us (11%)
  local copies, waits for them, and re-layouts  47.6 us (6%)
  between operations  13.8 us (2%)
    psum x1, blocking collectives, per_device(): back_all = lax.psum(back_part, 'tm').astype(jnp.bfloat16)  284 us
    psum x1, waiting for transfers between devices, per_device(): spectral = lax.psum(partial_spec, 'space')  216 us
    all_gather x1, waiting for transfers between devices, per_device(): lax.all_gather(series, 'tm', axis=2, tiled=True)  70.6 us
    all_gather x1, waiting for transfers between devices, per_device(): lax.all_gather(back_sub, 'space', axis=0, tiled=True)  39.1 us
    dot_general x1, matrix products, per_device(): jnp.dot(space_basis, scaled_spec, preferred_element_type=jnp.float32)  26.6 us
    dot_general x1, matrix products, per_device(): lax.dot_general(weighted, lax.all_gather(back_sub, 'space', axis=0, tiled...  25.5 us
    dot_general x1, matrix products, per_device(): lax.dot_general(space_basis, rotated, contract_rows, preferred_element_ty...  23.8 us
    all_gather x1, blocking collectives, per_device(): lax.all_gather(time_basis, 'tm', axis=0, tiled=True)  19 us
  transfers between devices with their start and end apart: 3, of which 3 were waited for; matrix products, arithmetic and copies ran while one was open for 2% of the time, Pallas kernels for 0%

commit v1 on v0

--- a/solution.py
+++ b/solution.py
@@ -34,7 +34,11 @@
     partial_spec = lax.dot_general(
         space_basis, rotated, contract_rows, preferred_element_type=jnp.float32
     )
-    spectral = lax.psum(partial_spec, "space")
+    spectral = partial_spec
+    for hop in (1, 2, 4):
+        spectral = spectral + lax.ppermute(
+            spectral, "space", [(dev, dev ^ hop) for dev in range(8)]
+        )
     eig_rows = lax.dynamic_slice_in_dim(space_eig, time_idx * col_block, col_block)
     scaled_spec = scale_block(spectral, eig_rows, cols_tiled)
     back_part = jnp.dot(space_basis, scaled_spec, preferred_element_type=jnp.float32)

time: 779 us -> 1330 us (1.71)
  waiting for transfers between devices: 327 us -> 847 us
  other arithmetic: 0 us -> 23.4 us
    ppermute x0 -> x3, waiting for transfers between devices: none -> 740 us  [per_device(): lax.ppermute(spectral, 'space', [(dev, dev ^ hop) for dev in range(8)])]
    psum x1 -> x0, waiting for transfers between devices: 216 us -> none  [per_device(): spectral = lax.psum(partial_spec, 'space')]
    add x0 -> x2, other arithmetic: none -> 23.4 us  [per_device(): spectral + lax.ppermute(spectral, 'space', [(dev, dev ^ hop) for dev in r...]
  transfers between devices with their start and end apart: 3 -> 5, of which waited for: 3 -> 5; matrix products, arithmetic and copies ran while one was open for 2% -> 1% of each run, Pallas kernels for 0% -> 0%
where the time goes in v1:
time: 1330 us
  waiting for transfers between devices  847 us (64%)
  blocking collectives  301 us (23%)
  matrix products  85.5 us (6%)
  local copies, waits for them, and re-layouts  53.8 us (4%)
  other arithmetic  23.4 us (2%)
  between operations  14.1 us (1%)
    ppermute x3, waiting for transfers between devices, per_device(): lax.ppermute(spectral, 'space', [(dev, dev ^ hop) for dev in range(8)])  740 us
    psum x1, blocking collectives, per_device(): back_all = lax.psum(back_part, 'tm').astype(jnp.bfloat16)  282 us
    all_gather x1, waiting for transfers between devices, per_device(): lax.all_gather(series, 'tm', axis=2, tiled=True)  70.6 us
    all_gather x1, waiting for transfers between devices, per_device(): lax.all_gather(back_sub, 'space', axis=0, tiled=True)  35.8 us
    dot_general x1, matrix products, per_device(): jnp.dot(space_basis, scaled_spec, preferred_element_type=jnp.float32)  26.7 us
  transfers between devices with their start and end apart: 5, of which 5 were waited for; matrix products, arithmetic and copies ran while one was open for 1% of the time, Pallas kernels for 0%

profile of v1, /device:TPU:0, one launch (start us, length us, event | category | flops | bytes accessed | tf_op | source)
XLA Modules:
  0.0 1327.4 jit_solution(1322161182806035810)
XLA Ops:
  8.0 19.0 %all_gather.10 = bf16[512,512]{1,0:T(8,128)(2,1)S(1)} all-gather(bf16[128,512]{1,0:T(8,128)(2,1)} %param.7), channel_id=1, replica_groups=mesh['space'=8,'tm'=4] {'tm'}, dimensions={0}, use_global_device_ids=true | all-gather | bytes 655360 | tf_op jit(solution)/shard_map/all_gather | solution.py:27
  27.0 70.6 %all-gather.3.cloned.1.call-done = bf16[2048,2,512]{2,1,0:T(2,128)(2,1)} async-done(((bf16[2048,2,128]{2,1,0:T(2,128)(2,1)}), bf16[2048,2,512]{2,1,0:T(2,128)(2,1)}) %all-gather.3.cloned.1.call-update) | async-done | bytes 4194320 | tf_op jit(solution)/shard_map/all_gather | solution.py:26
  97.5 7.2 reshape.26
  104.7 6.5 convolution_convert_fusion.1
  111.2 7.1 reshape.27
  118.3 22.5 %convolution_bitcast_fusion = f32[4096,1024]{0,1:T(8,128)S(1)} fusion(bf16[2048,1024]{1,0:T(8,128)(2,1)} %reshape.27, bf16[2048,4096]{1,0:T(8,128)(2,1)} %param.6), kind=kOutput, calls=%fused_computation.2 | convolution fusion | flops 17179869184 | bytes 37748736 | tf_op jit(solution)/shard_map/dot_general | solution.py:34
  140.8 6.1 copy-done.2
  146.9 19.2 %collective-permute-done = f32[4096,1024]{0,1:T(8,128)} collective-permute-done((f32[4096,1024]{0,1:T(8,128)S(1)}, f32[4096,1024]{0,1:T(8,128)}, u32[]{:S(2)}, u32[]{:S(2)}) %collective-permute-start) | collective-permute-done | bytes 16777248 | tf_op jit(solution)/shard_map/ppermute | solution.py:39
  166.1 11.4 add.23
  177.5 1.5 collective-permute-start.1
  178.9 361.0 %collective-permute-done.1 = f32[4096,1024]{0,1:T(8,128)} collective-permute-done((f32[4096,1024]{0,1:T(8,128)S(1)}, f32[4096,1024]{0,1:T(8,128)}, u32[]{:S(2)}, u32[]{:S(2)}) %collective-permute-start.1) | collective-permute-done | bytes 16777248 | tf_op jit(solution)/shard_map/ppermute | solution.py:39
  539.9 12.1 add.24
  552.0 1.4 collective-permute-start.2
  553.3 0.7 dynamic_slice.6
  554.0 359.6 %collective-permute-done.2 = f32[4096,1024]{0,1:T(8,128)} collective-permute-done((f32[4096,1024]{0,1:T(8,128)}, f32[4096,1024]{0,1:T(8,128)}, u32[]{:S(2)}, u32[]{:S(2)}) %collective-permute-start.2) | collective-permute-done | bytes 16777248 | tf_op jit(solution)/shard_map/ppermute | solution.py:39
  913.7 26.7 %fusion.1 = f32[2048,1024]{0,1:T(8,128)} fusion(bf16[2048,4096]{1,0:T(8,128)(2,1)} %param.6, f32[4096,1024]{0,1:T(8,128)} %add.24, f32[4096,1024]{0,1:T(8,128)} %collective-permute-done.2, f32[1024]{0:T(1024)S(1)} %bitcast.21, f32[4096]{0:T(1024)S(1)} %dynamic_slice.6), kind=kOutput, calls=%fused_computation.7 | convolution fusion | flops 17200840704 | bytes 58740736 | tf_op jit(solution)/shard_map/dot_general | solution.py:44
  940.3 281.7 %all-reduce.1 = bf16[2048,1024]{0,1:T(8,128)(2,1)} all-reduce(f32[2048,1024]{0,1:T(8,128)} %fusion.1), channel_id=1, replica_groups=mesh['space'=8,'tm'=4] {'tm'}, use_global_device_ids=true, to_apply=%region_0.0 | all-reduce | flops 2097152 | bytes 12582912 | tf_op jit(solution)/shard_map/psum | solution.py:45
  1222.0 2.4 constant_dynamic-slice_fusion
  1224.4 6.5 copy.7
  1230.9 7.2 reshape.28
  1238.1 4.4 convolution_convert_fusion.2
  1242.5 35.8 %all-gather.5.cloned.1.call-done = bf16[4096,1024]{0,1:T(8,128)(2,1)} async-done(((bf16[512,1024]{0,1:T(8,128)(2,1)}), bf16[4096,1024]{0,1:T(8,128)(2,1)}) %all-gather.5.cloned.1.call-update) | async-done | bytes 8388624 | tf_op jit(solution)/shard_map/all_gather | solution.py:61
  1278.4 25.5 %convolution_convert_fusion = bf16[2048,4096]{1,0:T(8,128)(2,1)} fusion(bf16[4096,1024]{0,1:T(8,128)(2,1)} %all-gather.5.cloned.1.call-done, bf16[2048,1024]{0,1:T(8,128)(2,1)} %all-reduce.1, f32[1024]{0:T(1024)S(1)} %bitcast.22), kind=kOutput, calls=%fused_computation.1 | convolution fusion | flops 17196646400 | bytes 29364224 | tf_op jit(solution)/shard_map/dot_general | solution.py:59
  1303.9 16.6 %copy.9 = bf16[256,8,8,512]{3,2,1,0:T(8,128)(2,1)} copy(bf16[256,8,8,512]{3,1,2,0:T(8,128)(2,1)} %bitcast.19) | data formatting | bytes 33554432
  (14 shorter events, 0.9 us)
Async XLA Ops:
  7.2 546.2 %copy-start = (f32[512]{0:T(512)S(1)}, f32[512]{0:T(512)}, u32[]{:S(2)}) copy-start(f32[512]{0:T(512)} %param.9) | copy-start | bytes 6148
  7.2 90.4 %all-gather.3.cloned.1.call-start = ((), (), s32[]{:S(2)}) async-start(), calls=%async_computation | async-start | bytes 5242880 | tf_op jit(solution)/shard_map/all_gather | solution.py:26
  7.9 1270.5 %all-gather.5.cloned.1.call-start = ((), (), s32[]{:S(2)}) async-start(), calls=%async_computation.1 | async-start | bytes 9437184 | tf_op jit(solution)/shard_map/all_gather | solution.py:61
  140.7 6.2 copy-start.2
  140.8 25.4 %collective-permute-start = (f32[4096,1024]{0,1:T(8,128)S(1)}, f32[4096,1024]{0,1:T(8,128)}, u32[]{:S(2)}, u32[]{:S(2)}) collective-permute-start(f32[4096,1024]{0,1:T(8,128)S(1)} %convolution_bitcast_fusion), channel_id=1, source_target_pairs={{0,4},{4,0},{8,12},{12,8},{16,20},{20,16},{24,28},{28,24},{1,5},{5... | collective-permute-start | bytes 50331656 | tf_op jit(solution)/shard_map/ppermute | solution.py:39
  177.5 362.4 %collective-permute-start.1 = (f32[4096,1024]{0,1:T(8,128)S(1)}, f32[4096,1024]{0,1:T(8,128)}, u32[]{:S(2)}, u32[]{:S(2)}) collective-permute-start(f32[4096,1024]{0,1:T(8,128)S(1)} %add.23), channel_id=1, source_target_pairs={{0,8},{4,12},{8,0},{12,4},{16,24},{20,28},{24,16},{28,20},{1,9},{5... | collective-permute-start | bytes 50331656 | tf_op jit(solution)/shard_map/ppermute | solution.py:39
  552.0 361.7 %collective-permute-start.2 = (f32[4096,1024]{0,1:T(8,128)}, f32[4096,1024]{0,1:T(8,128)}, u32[]{:S(2)}, u32[]{:S(2)}) collective-permute-start(f32[4096,1024]{0,1:T(8,128)} %add.24), channel_id=1, source_target_pairs={{0,16},{4,20},{8,24},{12,28},{16,0},{20,4},{24,8},{28,12},{1,17},{... | collective-permute-start | bytes 50331656 | tf_op jit(solution)/shard_map/ppermute | solution.py:39
  1224.4 13.7 %copy-start.3 = (bf16[128,512]{1,0:T(8,128)(2,1)S(1)}, bf16[128,512]{1,0:T(8,128)(2,1)}, u32[]{:S(2)}) copy-start(bf16[128,512]{1,0:T(8,128)(2,1)} %param.7) | copy-start | bytes 393220
  1303.9 16.6 %copy-start.1 = (f32[512]{0:T(512)S(1)}, f32[512]{0:T(512)}, u32[]{:S(2)}) copy-start(f32[512]{0:T(512)} %param.9) | copy-start | bytes 6148
Sparse Core Ops, SparseCore 0:
  9.5 87.9 all-gather.2
  1224.5 53.7 all-gather.4
